TPU v7x, 32 devices: a whole 2x2x4 slice. The times are simulated.
32 devices in a mesh: groups: 2 (over y), chan: 4 (over z), win: 2 (over x), sub: 2 (over core).
Axes of the slice: x: 2, y: 2, z: 4, core: 2. Of those that a mesh axis runs over, the one named last changes fastest.
Arguments:
- traces: bfloat16 [4, 2560, 1024], P(('groups', 'win'), 'chan'), parts along dimension 0, may hold values from -240 to 240, as said below
- channel_mask: int32 [5120], P(('groups', 'chan')), parts along dimension 0, may hold values 0 or 1
- smooth_width: int32 [512], replicated, may hold values from 1 to 16, as said below
- source_phase: int32 [8], P('groups'), parts along dimension 0, may hold values from 0 to 7
- pair_list: int32 [8, 5], P('groups'), parts along dimension 0, may hold values 0 or 1
Outputs:
- receiver_stack: float32 [8, 5, 101, 5120], P(('win', 'sub'), None, None, ('groups', 'chan')), parts along dimension 3
- source_stack: float32 [64, 5, 101, 640], P(('groups', 'chan', 'win', 'sub')), parts along dimension 0
There are 2 independent parts, one for each index of `groups`. A program takes and returns all parts, laid end to end along the dimension named above; an argument that names none is the same for every part. Nothing has to cross between parts.
Inputs may be any that keep to these rules, and one draw needn't show every extreme that they name: `traces`: float samples; each channel and each window has a scale of its own. `smooth_width`: every value from 1 to 16 may occur; 16 occurs in every draw.
All inputs are finite; a program needn't handle non-finite values. No bound on the sum of `channel_mask` on one device may be relied on, other than what follows from the above.
Results may differ from a plain program's by a relative error of at most 0.0052.
Values may be sent and summed in bfloat16 or wider, within the bound.
A program may use at most 192 MiB of HBM per device.

v0:
```python
import math

import jax
import jax.numpy as jnp
import numpy as np
from jax import lax
from jax.sharding import PartitionSpec as P

NB = 512
MAXLAG = 50
LAGS = 2 * MAXLAG + 1
ROWS = 112
STRIDE = 8
REACH = 2
VS = 8
OFFS = 5
FLOOR = 0.25


def from_behind(block, axis, distance):
    devices = range(lax.axis_size(axis))
    if distance % len(devices) == 0:
        return block
    route = [((i - distance) % len(devices), i) for i in devices]
    return lax.ppermute(block, axis, route)


def dft_rows(samples):
    phases = np.arange(NB)[:, None] * np.arange(samples)[None, :] % samples
    angles = phases * (2.0 * math.pi / samples)
    return jnp.asarray(np.concatenate([np.cos(angles), -np.sin(angles)], axis=0), jnp.bfloat16)


def lag_rows(samples):
    lags = np.zeros((2, ROWS), np.int64)
    lags[0, :LAGS] = np.arange(LAGS) - MAXLAG
    lags[1, :LAGS] = MAXLAG - np.arange(LAGS)
    phases = lags[:, :, None] * np.arange(NB) % samples
    angles = phases * (2.0 * math.pi / samples)
    return np.cos(angles).astype(np.float32), np.sin(angles).astype(np.float32)


def on_device(traces, channel_mask, smooth_width, source_phase, pair_list):
    windows, channels, samples = traces.shape
    sub_count = lax.axis_size("sub")
    win_count = lax.axis_size("win")
    blocks = lax.axis_size("chan")
    block_at = lax.axis_index("chan")
    total_windows = windows * win_count
    mine = VS // (win_count * sub_count)
    place = lax.axis_index("win") * sub_count + lax.axis_index("sub")
    scale = channel_mask.astype(jnp.float32) * samples ** (-0.5)

    spectrum = jnp.einsum(
        "mn,wcn->wmc", dft_rows(samples), traces, preferred_element_type=jnp.float32
    ) * scale
    spectrum = spectrum.reshape(windows, 2, NB, channels)
    amplitude = jnp.sqrt(spectrum[:, 0] ** 2 + spectrum[:, 1] ** 2)
    bins = jnp.arange(NB, dtype=jnp.int32)
    near = jnp.abs(bins[:, None] - bins[None, :]) <= smooth_width[:, None]
    weights = near.astype(jnp.bfloat16)
    count = jnp.sum(near.astype(jnp.float32), axis=1)
    high = amplitude.astype(jnp.bfloat16)
    low = (amplitude - high.astype(jnp.float32)).astype(jnp.bfloat16)
    total = jnp.einsum("kj,wjc->wkc", weights, high, preferred_element_type=jnp.float32)
    total = total + jnp.einsum("kj,wjc->wkc", weights, low, preferred_element_type=jnp.float32)
    smoothed = total / count[None, :, None]
    whitened = (spectrum / jnp.maximum(smoothed, FLOOR)[:, None]).astype(jnp.bfloat16)

    phase = source_phase[block_at]
    wanted = phase + STRIDE * jnp.arange(VS, dtype=jnp.int32)
    picker = (jnp.arange(channels, dtype=jnp.int32)[None, :] == wanted[:, None]).astype(jnp.bfloat16)
    own = jnp.einsum(
        "vc,wqkc->vwqk", picker, whitened, preferred_element_type=jnp.float32
    ).astype(jnp.bfloat16)
    own_all = jnp.concatenate([from_behind(own, "win", d) for d in range(win_count)], axis=1)
    own_mine = lax.dynamic_slice_in_dim(own_all, place * mine, mine, axis=0)
    spectra = jnp.concatenate([from_behind(whitened, "win", d) for d in range(win_count)], axis=0)
    spectra = spectra.reshape(total_windows * 2 * NB, channels)

    cosines, sines = lag_rows(samples)
    factor = (NB * total_windows) ** (-0.5)
    cosines = jnp.asarray(cosines * np.float32(factor))[None, :, :, None, :]
    sines = jnp.asarray(sines * np.float32(factor))[None, :, :, None, :]
    pieces = {}
    for offset in range(OFFS):
        key = (offset - REACH) % blocks
        if key in pieces:
            continue
        near_sources = from_behind(own_mine, "chan", key).astype(jnp.float32)
        re = near_sources[:, None, None, :, 0]
        im = near_sources[:, None, None, :, 1]
        turned = jnp.stack([re * cosines - im * sines, im * cosines + re * sines], axis=4)
        turned = turned.astype(jnp.bfloat16).reshape(mine * 2 * ROWS, total_windows * 2 * NB)
        lags = jnp.dot(turned, spectra, preferred_element_type=jnp.float32)
        lags = lags.reshape(mine, 2, ROWS, channels)
        sent = from_behind(lags[:, 1].astype(jnp.bfloat16), "chan", -key)
        pieces[key] = (lags[:, 0], sent)
    received, swapped = [], []
    for offset in range(OFFS):
        key = (offset - REACH) % blocks
        got = pair_list[(block_at - key) % blocks, offset].astype(jnp.float32)
        gave = pair_list[block_at, offset].astype(jnp.float32)
        received.append(pieces[key][0][:, :LAGS] * got)
        swapped.append(pieces[key][1][:, :LAGS].astype(jnp.float32) * gave)
    return jnp.stack(received, axis=1), jnp.stack(swapped, axis=1)


def solution(mesh):
    in_specs = (
        P(("groups", "win"), "chan", None),
        P(("groups", "chan")),
        P(),
        P("groups"),
        P("groups", None),
    )
    out_specs = (
        P(("win", "sub"), None, None, ("groups", "chan")),
        P(("groups", "chan", "win", "sub"), None, None, None),
    )
    return jax.shard_map(
        on_device, mesh=mesh, in_specs=in_specs, out_specs=out_specs, check_vma=False
    )
```

profile of v0, /device:TPU:9, one launch (start us, length us, event | category | flops | bytes accessed | tf_op | source)
XLA Modules:
  0.0 90.7 jit_solution(4182233193169397176)
XLA Ops:
  0.6 0.0 copy-start
  0.7 1.3 %dynamic_slice.36 = s32[1]{0:T(128)} dynamic-slice(s32[4]{0:T(128)} %param.11, s32[]{:T(128)S(6)} %select_n.45), dynamic_slice_sizes={1} | dynamic-slice | bytes 12 | tf_op jit(solution)/shard_map/dynamic_slice | solution.py:70
  2.0 0.6 multiply_add_fusion
  2.6 0.7 convert_multiply_fusion.2
  3.3 1.0 %convert_reduce_fusion = f32[512]{0:T(512)S(1)} fusion(s32[512]{0:T(512)} %param.10), kind=kLoop, calls=%fused_computation.46 | loop fusion | flops 1310208 | bytes 4096 | tf_op jit(solution)/shard_map/reduce_sum | solution.py:62
  4.3 0.0 copy-done
  4.3 0.0 copy-start.5
  4.3 3.4 %bitcast_multiply_fusion = f32[1,640,1024]{1,2,0:T(8,128)S(1)} fusion(bf16[1024,1024]{1,0:T(8,128)(2,1)} %constant.65.clone, bf16[1,640,1024]{2,1,0:T(8,128)(2,1)S(1)} %copy-done, f32[640]{0:T(1024)S(1)} %convert_multiply_fusion.2), kind=kOutput, calls=%fused_computation.3 | convolution fusion | flops 1342832640 | bytes 6031872 | tf_op jit(solution)/shard_map/mn,wcn->wmc/dot_general | solution.py:54
  7.8 0.0 copy-start.1
  7.8 0.0 copy-done.5
  7.8 1.1 %fusion.42 = f32[640,512]{1,0:T(8,128)S(1)} fusion(s32[512]{0:T(512)S(1)} %copy-done.5, f32[1,2,512,640]{3,2,1,0:T(8,128)S(1)} %bitcast.142), kind=kOutput, calls=%fused_computation.50 | convolution fusion | flops 337641472 | bytes 3934208 | tf_op jit(solution)/shard_map/kj,wjc->wkc/dot_general | solution.py:65
  8.8 0.4 copy-done.1
  9.3 2.2 %maximum_bitcast_fusion = f32[512,640]{0,1:T(8,128)} fusion(f32[640,512]{1,0:T(8,128)S(1)} %fusion.42, f32[512]{0:T(512)S(1)} %convert_reduce_fusion, s32[512]{0:T(512)S(1)} %copy-done.5, f32[1,2,512,640]{3,2,1,0:T(8,128)S(1)} %bitcast.143), kind=kOutput, calls=%fused_computation.41 | convolution fusion | flops 339607552 | bytes 5246976 | tf_op jit(solution)/shard_map/kj,wjc->wkc/dot_general | solution.py:66
  11.5 1.7 %copy.28 = f32[512,640]{1,0:T(8,128)S(1)} copy(f32[512,640]{0,1:T(8,128)} %maximum_bitcast_fusion) | data formatting | bytes 2621440 | tf_op jit(solution)/shard_map/div | solution.py:68
  13.2 0.0 copy-start.2
  13.2 2.3 %fusion.41 = bf16[8,1,2,512]{3,0,2,1:T(8,128)(2,1)S(1)} fusion(f32[2,512,640]{2,1,0:T(8,128)} %bitcast.144, f32[512,640]{1,0:T(8,128)S(1)} %copy.28, s32[8]{0:T(128)S(1)} %multiply_add_fusion), kind=kOutput, calls=%fused_computation.45 | convolution fusion | flops 11809792 | bytes 3948576 | tf_op jit(solution)/shard_map/vc,wqkc->vwqk/dot_general | solution.py:73
  15.5 0.0 copy-start.3
  15.5 0.0 copy-start.4
  15.6 1.2 %collective-permute-start = (bf16[8,1,2,512]{3,0,2,1:T(8,128)(2,1)S(1)}, bf16[8,1,2,512]{3,0,2,1:T(8,128)(2,1)}, u32[]{:S(2)}, u32[]{:S(2)}) collective-permute-start(bf16[8,1,2,512]{3,0,2,1:T(8,128)(2,1)S(1)} %fusion.41), channel_id=1, source_target_pairs={{2,0},{0,2},{3,1},{1,3},{6,4},{4,6},{7,5},{5,7},{10,8},{8,10},{11,... | collective-permute-start | bytes 49160 | tf_op jit(solution)/shard_map/ppermute | solution.py:25
  16.8 0.0 copy-done.2
  16.8 1.3 %divide_convert_fusion = bf16[1,2,512,640]{3,2,1,0:T(8,128)(2,1)} fusion(f32[1,2,512,640]{3,2,1,0:T(8,128)S(1)} %bitcast.145, f32[512,640]{1,0:T(8,128)S(1)} %copy.28), kind=kLoop, calls=%fused_computation.10 | loop fusion | flops 1310720 | bytes 5242880 | tf_op jit(solution)/shard_map/convert_element_type | solution.py:68
  18.1 0.3 collective-permute-start.2
  18.4 1.7 %constant_dynamic-slice_fusion.8 = (s32[1,1]{1,0:T(1,128)}, s32[1,1]{1,0:T(1,128)}, s32[1,1]{1,0:T(1,128)}, s32[1,1]{1,0:T(1,128)}, s32[1,1]{1,0:T(1,128)}, /*in...) fusion(s32[4,5]{1,0:T(4,128)} %param.12, s32[]{:T(128)S(6)} %select_n.45, ...), kind=kLoop, calls=%fused_computation.109 | loop fusion | bytes 100 | tf_op jit(solution)/shard_map/dynamic_slice | solution.py:103
  26.4 0.0 collective-permute-done
  26.4 0.7 fusion.68
  27.2 2.4 %collective-permute-start.1 = (bf16[2,2,2,512]{3,0,2,1:T(2,128)(2,1)S(1)}, bf16[2,2,2,512]{3,0,2,1:T(2,128)(2,1)S(1)}, u32[]{:S(2)}, u32[]{:S(2)}) collective-permute-start(bf16[2,2,2,512]{3,0,2,1:T(2,128)(2,1)S(1)} %get-tuple-element.7), channel_id=1, source_target_pairs={{8,0},{12,4},{0,8},{4,12},{9,1},{13,5},{1,9},{5,13},{10,2},{14,6},... | collective-permute-start | bytes 24584 | tf_op jit(solution)/shard_map/ppermute | solution.py:25
  29.6 0.2 collective-permute-start.3
  29.7 1.3 %collective-permute-start.4 = (bf16[2,2,2,512]{3,0,2,1:T(2,128)(2,1)S(1)}, bf16[2,2,2,512]{3,0,2,1:T(2,128)(2,1)S(1)}, u32[]{:S(2)}, u32[]{:S(2)}) collective-permute-start(bf16[2,2,2,512]{3,0,2,1:T(2,128)(2,1)S(1)} %get-tuple-element.7), channel_id=1, source_target_pairs={{12,0},{0,4},{4,8},{8,12},{13,1},{1,5},{5,9},{9,13},{14,2},{2,6},{... | collective-permute-start | bytes 24584 | tf_op jit(solution)/shard_map/ppermute | solution.py:25
  31.1 0.0 collective-permute-done.1
  31.1 1.3 %collective-permute-done.3 = bf16[2,2,2,512]{3,0,2,1:T(2,128)(2,1)S(1)} collective-permute-done((bf16[2,2,2,512]{3,0,2,1:T(2,128)(2,1)S(1)}, bf16[2,2,2,512]{3,0,2,1:T(2,128)(2,1)S(1)}, u32[]{:S(2)}, u32[]{:S(2)}) %collective-permute-start.3) | collective-permute-done | bytes 8224 | tf_op jit(solution)/shard_map/ppermute | solution.py:25
  32.4 0.1 collective-permute-done.4
  32.6 0.0 copy-done.3
  32.6 0.0 copy-done.4
  32.6 2.2 %subtract_convert_fusion = (bf16[2,2,112,2,1,512]{5,2,4,3,1,0:T(8,128)(2,1)S(1)}, bf16[2,2,112,2,1,512]{5,2,4,3,1,0:T(8,128)(2,1)S(1)}, bf16[2,2,112,2,1,512]{5,...) fusion(f32[2,2,512]{2,1,0:T(2,128)S(1)} %copy.39, ...), kind=kLoop, calls=%fused_computation.22 | loop fusion | flops 14680064 | bytes 8323072 | tf_op jit(solution)/shard_map/convert.4
  34.8 0.3 pad_maximum_fusion.1
  35.2 12.5 %collective-permute-done.2 = bf16[1,2,512,640]{3,2,1,0:T(8,128)(2,1)S(1)} collective-permute-done((bf16[1,2,512,640]{3,2,1,0:T(8,128)(2,1)}, bf16[1,2,512,640]{3,2,1,0:T(8,128)(2,1)S(1)}, u32[]{:S(2)}, u32[]{:S(2)}) %collective-permute-start.2) | collective-permute-done | bytes 1310752 | tf_op jit(solution)/shard_map/ppermute | solution.py:25
  47.6 2.9 %fusion.15 = f32[2,2,112,640]{3,2,0,1:T(8,128)S(1)} fusion(bf16[1,2,512,640]{3,2,1,0:T(8,128)(2,1)S(1)} %collective-permute-done.2, bf16[1,2,512,640]{3,2,1,0:T(8,128)(2,1)} %divide_convert_fusion, bf16[2,2,112,2,1,512]{5,2,4,3,1,0:T(8,128)(2,1)S(1)} %get-tuple-element.9, bf16[2,2,112,2,1,512]{5,2,4,3,1,0:T(8,128)(2,1)S(1)} %get-tuple-element.8), kind=kOutput, calls=%fused_computation.31 | convolution fusion | flops 1176633344 | bytes 5603328 | tf_op jit(solution)/shard_map/dot_general | solution.py:95
  50.6 2.9 %fusion.25 = f32[2,2,112,640]{3,2,0,1:T(8,128)S(1)} fusion(bf16[2,2,112,2,2,512]{5,2,4,3,1,0:T(8,128)(2,1)S(1)} %get-tuple-element.41, bf16[1,2,512,640]{3,2,1,0:T(8,128)(2,1)S(1)} %collective-permute-done.2, bf16[1,2,512,640]{3,2,1,0:T(8,128)(2,1)} %divide_convert_fusion), kind=kOutput, calls=%fused_computation.33 | convolution fusion | flops 1175715840 | bytes 5603328 | tf_op jit(solution)/shard_map/dot_general | solution.py:95
  53.6 2.9 %fusion.20 = f32[2,2,112,640]{3,2,0,1:T(8,128)S(1)} fusion(bf16[2,2,112,2,2,512]{5,2,4,3,1,0:T(8,128)(2,1)S(1)} %get-tuple-element.40, bf16[1,2,512,640]{3,2,1,0:T(8,128)(2,1)S(1)} %collective-permute-done.2, bf16[1,2,512,640]{3,2,1,0:T(8,128)(2,1)} %divide_convert_fusion), kind=kOutput, calls=%fused_computation.32 | convolution fusion | flops 1175715840 | bytes 5603328 | tf_op jit(solution)/shard_map/dot_general | solution.py:95
  56.7 2.9 %fusion.30 = f32[2,2,112,640]{3,2,1,0:T(8,128)S(1)} fusion(bf16[2,2,112,2,1,512]{5,2,4,3,1,0:T(8,128)(2,1)S(1)} %get-tuple-element.20, bf16[2,2,112,2,1,512]{5,2,4,3,1,0:T(8,128)(2,1)S(1)} %get-tuple-element.21, bf16[1,2,512,640]{3,2,1,0:T(8,128)(2,1)S(1)} %collective-permute-done.2, bf16[1,2,512,640]{3,2,1,0:T(8,128)(2,1)} %divide_convert_fusion), kind=kOutput, calls=%fused_computation.34 | convolution fusion | flops 1176633344 | bytes 5603328 | tf_op jit(solution)/shard_map/dot_general | solution.py:95
  59.7 1.4 %collective-permute-start.6 = (bf16[2,112,640]{2,1,0:T(8,128)(2,1)S(1)}, bf16[2,112,640]{2,1,0:T(8,128)(2,1)S(1)}, u32[]{:S(2)}, u32[]{:S(2)}) collective-permute-start(bf16[2,112,640]{2,1,0:T(8,128)(2,1)S(1)} %fusion.58), channel_id=1, source_target_pairs={{12,0},{0,4},{4,8},{8,12},{13,1},{1,5},{5,9},{9,13},{14,2},{2,6},{... | collective-permute-start | bytes 860168 | tf_op jit(solution)/shard_map/ppermute | solution.py:25
  61.0 1.1 %collective-permute-start.5 = (bf16[2,112,640]{2,1,0:T(8,128)(2,1)S(1)}, bf16[2,112,640]{2,1,0:T(8,128)(2,1)S(1)}, u32[]{:S(2)}, u32[]{:S(2)}) collective-permute-start(bf16[2,112,640]{2,1,0:T(8,128)(2,1)S(1)} %fusion.57), channel_id=1, source_target_pairs={{8,0},{12,4},{0,8},{4,12},{9,1},{13,5},{1,9},{5,13},{10,2},{14,6},... | collective-permute-start | bytes 860168 | tf_op jit(solution)/shard_map/ppermute | solution.py:25
  62.1 1.4 %collective-permute-start.7 = (bf16[2,112,640]{2,1,0:T(8,128)(2,1)S(1)}, bf16[2,112,640]{2,1,0:T(8,128)(2,1)S(1)}, u32[]{:S(2)}, u32[]{:S(2)}) collective-permute-start(bf16[2,112,640]{2,1,0:T(8,128)(2,1)S(1)} %fusion.60), channel_id=1, source_target_pairs={{4,0},{8,4},{12,8},{0,12},{5,1},{9,5},{13,9},{1,13},{6,2},{10,6},{... | collective-permute-start | bytes 860168 | tf_op jit(solution)/shard_map/ppermute | solution.py:25
  63.8 2.8 %copy.44 = f32[2,5,101,640]{3,0,2,1:T(2,128)} copy(f32[2,5,101,640]{3,2,0,1:T(8,128)S(1)} %bitcast_dynamic-update-slice_fusion.3) | data formatting | bytes 5171200
  66.6 17.1 %collective-permute-done.5 = bf16[2,112,640]{2,1,0:T(8,128)(2,1)S(1)} collective-permute-done((bf16[2,112,640]{2,1,0:T(8,128)(2,1)S(1)}, bf16[2,112,640]{2,1,0:T(8,128)(2,1)S(1)}, u32[]{:S(2)}, u32[]{:S(2)}) %collective-permute-start.5) | collective-permute-done | bytes 286752 | tf_op jit(solution)/shard_map/ppermute | solution.py:25
  83.7 0.0 collective-permute-done.6
  83.9 4.0 %collective-permute-done.7 = bf16[2,112,640]{2,1,0:T(8,128)(2,1)S(1)} collective-permute-done((bf16[2,112,640]{2,1,0:T(8,128)(2,1)S(1)}, bf16[2,112,640]{2,1,0:T(8,128)(2,1)S(1)}, u32[]{:S(2)}, u32[]{:S(2)}) %collective-permute-start.7) | collective-permute-done | bytes 286752 | tf_op jit(solution)/shard_map/ppermute | solution.py:25
  87.9 2.8 %copy.45 = f32[2,5,101,640]{3,0,2,1:T(2,128)} copy(f32[2,5,101,640]{3,2,0,1:T(8,128)S(1)} %fusion.46) | data formatting | bytes 5171200
  (33 shorter events, 0.8 us)
Async XLA Ops:
  0.6 3.7 %copy-start = (bf16[1,640,1024]{2,1,0:T(8,128)(2,1)S(1)}, bf16[1,640,1024]{2,1,0:T(8,128)(2,1)}, u32[]{:S(2)}) copy-start(bf16[1,640,1024]{2,1,0:T(8,128)(2,1)} %param.8) | copy-start | bytes 3932164
  4.3 3.5 %copy-start.5 = (s32[512]{0:T(512)S(1)}, s32[512]{0:T(512)}, u32[]{:S(2)}) copy-start(s32[512]{0:T(512)} %param.10) | copy-start | bytes 6148
  7.8 1.5 %copy-start.1 = (f32[1,640,1024]{1,2,0:T(8,128)}, f32[1,640,1024]{1,2,0:T(8,128)S(1)}, u32[]{:S(2)}) copy-start(f32[1,640,1024]{1,2,0:T(8,128)S(1)} %bitcast_multiply_fusion) | copy-start | bytes 7864324
  13.2 3.6 %copy-start.2 = (f32[1,640,1024]{1,2,0:T(8,128)S(1)}, f32[1,640,1024]{1,2,0:T(8,128)}, u32[]{:S(2)}) copy-start(f32[1,640,1024]{1,2,0:T(8,128)} %copy-done.1) | copy-start | bytes 7864324
  15.5 17.0 %copy-start.3 = (f32[2,112,512]{2,1,0:T(8,128)S(1)}, f32[2,112,512]{2,1,0:T(8,128)}, u32[]{:S(2)}) copy-start(f32[2,112,512]{2,1,0:T(8,128)} %constant.66.clone) | copy-start | bytes 1376260
  15.5 17.0 %copy-start.4 = (f32[2,112,512]{2,1,0:T(8,128)S(1)}, f32[2,112,512]{2,1,0:T(8,128)}, u32[]{:S(2)}) copy-start(f32[2,112,512]{2,1,0:T(8,128)} %constant.67.clone) | copy-start | bytes 1376260
  15.6 10.9 %collective-permute-start = (bf16[8,1,2,512]{3,0,2,1:T(8,128)(2,1)S(1)}, bf16[8,1,2,512]{3,0,2,1:T(8,128)(2,1)}, u32[]{:S(2)}, u32[]{:S(2)}) collective-permute-start(bf16[8,1,2,512]{3,0,2,1:T(8,128)(2,1)S(1)} %fusion.41), channel_id=1, source_target_pairs={{2,0},{0,2},{3,1},{1,3},{6,4},{4,6},{7,5},{5,7},{10,8},{8,10},{11,... | collective-permute-start | bytes 49160 | tf_op jit(solution)/shard_map/ppermute | solution.py:25
  18.1 29.5 %collective-permute-start.2 = (bf16[1,2,512,640]{3,2,1,0:T(8,128)(2,1)}, bf16[1,2,512,640]{3,2,1,0:T(8,128)(2,1)S(1)}, u32[]{:S(2)}, u32[]{:S(2)}) collective-permute-start(bf16[1,2,512,640]{3,2,1,0:T(8,128)(2,1)} %divide_convert_fusion), channel_id=1, source_target_pairs={{2,0},{0,2},{3,1},{1,3},{6,4},{4,6},{7,5},{5,7},{10,8},{8,10},{11,... | collective-permute-start | bytes 3932168 | tf_op jit(solution)/shard_map/ppermute | solution.py:25
  27.2 3.9 %collective-permute-start.1 = (bf16[2,2,2,512]{3,0,2,1:T(2,128)(2,1)S(1)}, bf16[2,2,2,512]{3,0,2,1:T(2,128)(2,1)S(1)}, u32[]{:S(2)}, u32[]{:S(2)}) collective-permute-start(bf16[2,2,2,512]{3,0,2,1:T(2,128)(2,1)S(1)} %get-tuple-element.7), channel_id=1, source_target_pairs={{8,0},{12,4},{0,8},{4,12},{9,1},{13,5},{1,9},{5,13},{10,2},{14,6},... | collective-permute-start | bytes 24584 | tf_op jit(solution)/shard_map/ppermute | solution.py:25
  29.6 2.8 %collective-permute-start.3 = (bf16[2,2,2,512]{3,0,2,1:T(2,128)(2,1)S(1)}, bf16[2,2,2,512]{3,0,2,1:T(2,128)(2,1)S(1)}, u32[]{:S(2)}, u32[]{:S(2)}) collective-permute-start(bf16[2,2,2,512]{3,0,2,1:T(2,128)(2,1)S(1)} %get-tuple-element.7), channel_id=1, source_target_pairs={{4,0},{8,4},{12,8},{0,12},{5,1},{9,5},{13,9},{1,13},{6,2},{10,6},{... | collective-permute-start | bytes 24584 | tf_op jit(solution)/shard_map/ppermute | solution.py:25
  29.7 2.8 %collective-permute-start.4 = (bf16[2,2,2,512]{3,0,2,1:T(2,128)(2,1)S(1)}, bf16[2,2,2,512]{3,0,2,1:T(2,128)(2,1)S(1)}, u32[]{:S(2)}, u32[]{:S(2)}) collective-permute-start(bf16[2,2,2,512]{3,0,2,1:T(2,128)(2,1)S(1)} %get-tuple-element.7), channel_id=1, source_target_pairs={{12,0},{0,4},{4,8},{8,12},{13,1},{1,5},{5,9},{9,13},{14,2},{2,6},{... | collective-permute-start | bytes 24584 | tf_op jit(solution)/shard_map/ppermute | solution.py:25
  59.7 24.1 %collective-permute-start.6 = (bf16[2,112,640]{2,1,0:T(8,128)(2,1)S(1)}, bf16[2,112,640]{2,1,0:T(8,128)(2,1)S(1)}, u32[]{:S(2)}, u32[]{:S(2)}) collective-permute-start(bf16[2,112,640]{2,1,0:T(8,128)(2,1)S(1)} %fusion.58), channel_id=1, source_target_pairs={{12,0},{0,4},{4,8},{8,12},{13,1},{1,5},{5,9},{9,13},{14,2},{2,6},{... | collective-permute-start | bytes 860168 | tf_op jit(solution)/shard_map/ppermute | solution.py:25
  61.0 22.7 %collective-permute-start.5 = (bf16[2,112,640]{2,1,0:T(8,128)(2,1)S(1)}, bf16[2,112,640]{2,1,0:T(8,128)(2,1)S(1)}, u32[]{:S(2)}, u32[]{:S(2)}) collective-permute-start(bf16[2,112,640]{2,1,0:T(8,128)(2,1)S(1)} %fusion.57), channel_id=1, source_target_pairs={{8,0},{12,4},{0,8},{4,12},{9,1},{13,5},{1,9},{5,13},{10,2},{14,6},... | collective-permute-start | bytes 860168 | tf_op jit(solution)/shard_map/ppermute | solution.py:25
  62.1 25.7 %collective-permute-start.7 = (bf16[2,112,640]{2,1,0:T(8,128)(2,1)S(1)}, bf16[2,112,640]{2,1,0:T(8,128)(2,1)S(1)}, u32[]{:S(2)}, u32[]{:S(2)}) collective-permute-start(bf16[2,112,640]{2,1,0:T(8,128)(2,1)S(1)} %fusion.60), channel_id=1, source_target_pairs={{4,0},{8,4},{12,8},{0,12},{5,1},{9,5},{13,9},{1,13},{6,2},{10,6},{... | collective-permute-start | bytes 860168 | tf_op jit(solution)/shard_map/ppermute | solution.py:25
where the time goes:
time: 91.3 us; the launch traced here: 90.7 us
  waiting for transfers between devices  35 us (38%)
  matrix products  20.7 us (23%)
  local copies, waits for them, and re-layouts  11.2 us (12%)
  starting transfers between devices  9.18 us (10%)
  other arithmetic  7.37 us (8%)
  between operations  7.33 us (8%)
    ppermute x8, waiting for transfers between devices, from_behind(): return lax.ppermute(block, axis, route)  35 us
    dot_general x4, matrix products, on_device(): lags = jnp.dot(turned, spectra, preferred_element_type=jnp.float32)  11.6 us
    ppermute x8, starting transfers between devices, from_behind(): return lax.ppermute(block, axis, route)  9.18 us
    unnamed x14, local copies, waits for them, and re-layouts  6.08 us
    dot_general x1, matrix products, on_device(): jnp.einsum('mn,wcn->wmc', dft_rows(samples), traces, preferred_element_ty...  3.42 us
    dot_general x1, matrix products, on_device(): jnp.einsum('vc,wqkc->vwqk', picker, whitened, preferred_element_type=jnp....  2.34 us
    another operation x1, other arithmetic  2.23 us
    dot_general x1, matrix products, on_device(): jnp.einsum('kj,wjc->wkc', weights, low, preferred_element_type=jnp.float32)  2.21 us
  transfers between devices with their start and end apart: 8, of which 5 were waited for; matrix products, arithmetic and copies ran while one was open for 11% of the time, Pallas kernels for 0%

commit v1 on v0

v1 whole, which is shorter than its diff:
```python
import functools
import math

import jax
import jax.numpy as jnp
import numpy as np
from jax import lax
from jax.experimental import pallas as pl
from jax.experimental.pallas import tpu as pltpu
from jax.sharding import PartitionSpec as P

NB = 512
MAXLAG = 50
LAGS = 2 * MAXLAG + 1
SLOT = 104
STRIDE = 8
REACH = 2
VS = 8
OFFS = 5
FLOOR = 0.25
MESH = pl.DeviceIdType.MESH
FAR = (((1,), (1,)), ((), ()))


def dft_rows(samples):
    phases = np.arange(NB)[:, None] * np.arange(samples)[None, :] % samples
    angles = phases * (2.0 * math.pi / samples)
    return jnp.asarray(np.concatenate([np.cos(angles), -np.sin(angles)], axis=0), jnp.bfloat16)


def lag_rows(samples, factor):
    lags = np.zeros((SLOT,), np.int64)
    lags[:LAGS] = np.arange(LAGS) - MAXLAG
    angles = (lags[:, None] * np.arange(NB) % samples) * (2.0 * math.pi / samples)
    tables = np.stack([np.cos(angles), np.sin(angles)]) * factor
    return jnp.asarray(tables, jnp.float32)


def chunks_of(channels):
    cuts = [(0, 128)]
    while sum(cuts[-1]) < channels:
        start = sum(cuts[-1])
        cuts.append((start, min(256, channels - start)))
    return cuts


def kernel(keys, wins, subs, mine, rows, cuts, *refs):
    phase_ref, traces, mask, widths, dft, lag = refs[:6]
    fwd, own_back, far_back = refs[6:9]
    count = len(cuts)
    spectra = refs[9 : 9 + count]
    staged = refs[9 + count : 9 + 2 * count]
    (weights, own_sources, sources, far_rows, near_rows,
     s_send, s_recv, x_send, x_recv, c_send, c_recv, z_send, z_recv) = refs[9 + 2 * count :]
    samples = traces.shape[1]
    blocks = lax.axis_size("chan")
    block_at = lax.axis_index("chan")
    win_at = lax.axis_index("win")
    sub_at = lax.axis_index("sub")
    sub_peer = {"sub": 1 - sub_at}

    def peer(key, d):
        return {"chan": lax.rem(block_at + key, blocks), "win": lax.rem(win_at + d, wins)}

    others = [(key, d) for key in keys for d in range(wins) if (key, d) != (0, 0)]
    barrier = pltpu.get_barrier_semaphore()
    for key, d in others:
        pl.semaphore_signal(barrier, inc=1, device_id=peer(key, d), device_id_type=MESH)
    pl.semaphore_signal(barrier, inc=1, device_id=sub_peer, device_id_type=MESH)

    width_row = widths[...].astype(jnp.float32)
    width_col = jnp.transpose(jnp.broadcast_to(width_row, (128, NB)))[:, :1]
    at = lax.broadcasted_iota(jnp.int32, (NB, NB), 0)
    to = lax.broadcasted_iota(jnp.int32, (NB, NB), 1)
    near = jnp.abs(at - to).astype(jnp.float32) <= width_col
    weights[...] = jnp.where(near, 1.0, 0.0).astype(jnp.bfloat16)
    bins = lax.broadcasted_iota(jnp.int32, (NB, 1), 0).astype(jnp.float32)
    inside = jnp.minimum(bins + width_col, NB - 1.0) - jnp.maximum(bins - width_col, 0.0) + 1.0
    share = 1.0 / inside

    def whiten(i):
        start, width = cuts[i]
        cut = traces[start : start + width, :]
        scale = mask[:, start : start + width].astype(jnp.float32) * samples ** (-0.5)
        re = lax.dot_general(dft[:NB, :], cut, FAR, preferred_element_type=jnp.float32) * scale
        im = lax.dot_general(dft[NB:, :], cut, FAR, preferred_element_type=jnp.float32) * scale
        amplitude = jnp.sqrt(re * re + im * im)
        high = amplitude.astype(jnp.bfloat16)
        low = (amplitude - high.astype(jnp.float32)).astype(jnp.bfloat16)
        total = jnp.dot(weights[...], high, preferred_element_type=jnp.float32)
        total = total + jnp.dot(weights[...], low, preferred_element_type=jnp.float32)
        gain = 1.0 / jnp.maximum(total * share, FLOOR)
        spectra[i][:NB, :] = (re * gain).astype(jnp.bfloat16)
        spectra[i][NB : 2 * NB, :] = (im * gain).astype(jnp.bfloat16)

    def x_copies(i):
        src = pl.ds(pl.multiple_of(sub_at * NB, NB), NB)
        copies = []
        for d in range(1, wins):
            dst = pl.ds(pl.multiple_of(d * 2 * NB + sub_at * NB, NB), NB)
            copies.append(pltpu.make_async_remote_copy(
                src_ref=spectra[i].at[src], dst_ref=spectra[i].at[dst],
                send_sem=x_send.at[i, d - 1], recv_sem=x_recv.at[i, d - 1],
                device_id={"win": lax.rem(win_at + d, wins)}, device_id_type=MESH))
        return copies

    def c_copies(i):
        copies = []
        for d in range(1, wins):
            part = pl.ds(pl.multiple_of(d * 2 * NB + sub_at * NB, NB), NB)
            copies.append(pltpu.make_async_remote_copy(
                src_ref=spectra[i].at[part], dst_ref=spectra[i].at[part],
                send_sem=c_send.at[i, d - 1], recv_sem=c_recv.at[i, d - 1],
                device_id=sub_peer, device_id_type=MESH))
        return copies

    def z_copies(i):
        start, width = cuts[i]
        copies = []
        for n, key in enumerate(keys[1:]):
            copies.append(pltpu.make_async_remote_copy(
                src_ref=staged[i].at[n], dst_ref=far_back.at[n, :, start : start + width],
                send_sem=z_send.at[i, n], recv_sem=z_recv.at[i, n],
                device_id={"chan": lax.rem(block_at + blocks - key, blocks)}, device_id_type=MESH))
        return copies

    whiten(0)
    phase = phase_ref[block_at]
    row_ids = lax.broadcasted_iota(jnp.int32, (16, cuts[0][1]), 0)
    lane_ids = lax.broadcasted_iota(jnp.int32, (16, cuts[0][1]), 1)
    chosen = (lane_ids == phase + STRIDE * row_ids) & (row_ids < VS)
    picker = jnp.where(chosen, 1.0, 0.0).astype(jnp.bfloat16)
    picked = lax.dot_general(
        picker, spectra[0][: 2 * NB, :], FAR, preferred_element_type=jnp.float32)
    for v in range(VS):
        own_sources[v // mine, v % mine : v % mine + 1, :] = picked[v : v + 1, :]
    sources[0, 0] = own_sources[win_at * subs + sub_at]
    pl.semaphore_wait(barrier, len(others) + 1)

    s_copies = []
    for key, d in others:
        n = keys.index(key)
        s_copies.append(pltpu.make_async_remote_copy(
            src_ref=own_sources.at[lax.rem(win_at + d, wins) * subs + sub_at],
            dst_ref=sources.at[n, d],
            send_sem=s_send.at[n, d], recv_sem=s_recv.at[n, d],
            device_id=peer(key, d), device_id_type=MESH))
    for copy in s_copies:
        copy.start()
    over_x, over_c, over_z = [x_copies(0)], [], []
    for copy in over_x[0]:
        copy.start()
    for i in range(1, count):
        whiten(i)
        over_x.append(x_copies(i))
        for copy in over_x[i]:
            copy.start()

    def forward(i):
        over_c.append(c_copies(i))
        for arrived, onward in zip(over_x[i], over_c[i]):
            arrived.wait_recv()
            onward.start()

    forward(0)
    for copy in s_copies:
        copy.wait_recv()
    blank = rows - mine * SLOT

    def fill(target, at_row, sign, n, d):
        re_parts, im_parts = [], []
        for v in range(mine):
            re = sources[n, d, v : v + 1, :NB]
            im = sources[n, d, v : v + 1, NB:]
            cosines, sines = lag[0], lag[1] * sign
            re_parts.append(re * cosines - im * sines)
            im_parts.append(im * cosines + re * sines)
        if blank:
            re_parts.append(jnp.zeros((blank, NB), jnp.float32))
            im_parts.append(jnp.zeros((blank, NB), jnp.float32))
        base = d * 2 * NB
        span = slice(at_row, at_row + rows)
        target[span, base : base + NB] = jnp.concatenate(re_parts, axis=0).astype(jnp.bfloat16)
        target[span, base + NB : base + 2 * NB] = jnp.concatenate(im_parts, axis=0).astype(jnp.bfloat16)

    for n in range(1, len(keys)):
        for d in range(wins):
            fill(far_rows, (n - 1) * rows, -1.0, n, d)

    def send(i):
        for copy in over_c[i]:
            copy.wait_recv()
        lags = jnp.dot(far_rows[...], spectra[i][...], preferred_element_type=jnp.float32)
        for n in range(len(keys) - 1):
            staged[i][n] = lags[n * rows : (n + 1) * rows].astype(jnp.bfloat16)
        over_z.append(z_copies(i))
        for copy in over_z[i]:
            copy.start()

    def keep(i):
        start, width = cuts[i]
        lags = jnp.dot(near_rows[...], spectra[i][...], preferred_element_type=jnp.float32)
        for n in range(len(keys)):
            fwd[n, :, start : start + width] = lags[n * rows : (n + 1) * rows].astype(jnp.bfloat16)
        own_back[:, start : start + width] = lags[len(keys) * rows :].astype(jnp.bfloat16)

    send(0)
    for i in range(1, count):
        forward(i)
        if i == 1:
            for d in range(wins):
                for n in range(len(keys)):
                    fill(near_rows, n * rows, 1.0, n, d)
                fill(near_rows, len(keys) * rows, -1.0, 0, d)
        send(i)
    for i in range(count):
        keep(i)
    for copies in over_z:
        for copy in copies:
            copy.wait()
    for copies in over_x + over_c + [s_copies]:
        for copy in copies:
            copy.wait_send()


def on_device(traces, channel_mask, smooth_width, source_phase, pair_list):
    windows, channels, samples = traces.shape
    subs = lax.axis_size("sub")
    wins = lax.axis_size("win")
    blocks = lax.axis_size("chan")
    block_at = lax.axis_index("chan")
    mine = VS // (wins * subs)
    rows = -(-mine * SLOT // 16) * 16
    keys = [0]
    for offset in range(OFFS):
        key = (offset - REACH) % blocks
        if key not in keys:
            keys.append(key)
    nk = len(keys)
    depth = wins * 2 * NB
    cuts = chunks_of(channels)
    count = len(cuts)
    vmem = pl.BlockSpec(memory_space=pltpu.VMEM)
    dma = pltpu.SemaphoreType.DMA
    fwd, own_back, far_back = pl.pallas_call(
        functools.partial(kernel, keys, wins, subs, mine, rows, cuts),
        out_shape=[
            jax.ShapeDtypeStruct((nk, rows, channels), jnp.bfloat16),
            jax.ShapeDtypeStruct((rows, channels), jnp.bfloat16),
            jax.ShapeDtypeStruct((nk - 1, rows, channels), jnp.bfloat16),
        ],
        in_specs=[pl.BlockSpec(memory_space=pltpu.SMEM)] + [vmem] * 5,
        out_specs=[vmem, vmem, pl.BlockSpec(memory_space=pl.ANY)],
        scratch_shapes=[pltpu.VMEM((depth, width), jnp.bfloat16) for _, width in cuts]
        + [pltpu.VMEM((nk - 1, rows, width), jnp.bfloat16) for _, width in cuts]
        + [
            pltpu.VMEM((NB, NB), jnp.bfloat16),
            pltpu.VMEM((wins * subs, mine, 2 * NB), jnp.float32),
            pltpu.VMEM((nk, wins, mine, 2 * NB), jnp.float32),
            pltpu.VMEM(((nk - 1) * rows, depth), jnp.bfloat16),
            pltpu.VMEM(((nk + 1) * rows, depth), jnp.bfloat16),
            dma((nk, wins)), dma((nk, wins)),
            dma((count, wins - 1)), dma((count, wins - 1)),
            dma((count, wins - 1)), dma((count, wins - 1)),
            dma((count, nk - 1)), dma((count, nk - 1)),
        ],
        compiler_params=pltpu.CompilerParams(
            collective_id=0, has_side_effects=True, vmem_limit_bytes=56 * 2**20
        ),
        name="stacks",
    )(
        source_phase,
        traces.reshape(channels, samples),
        channel_mask.reshape(1, channels),
        smooth_width.reshape(1, NB),
        dft_rows(samples),
        lag_rows(samples, (NB * windows * wins) ** (-0.5)),
    )
    received, swapped = [], []
    for offset in range(OFFS):
        key = (offset - REACH) % blocks
        n = keys.index(key)
        got = pair_list[(block_at - key) % blocks, offset].astype(jnp.float32)
        gave = pair_list[block_at, offset].astype(jnp.float32)
        back = own_back if n == 0 else far_back[n - 1]
        for stack, cells, paired in ((received, fwd[n], got), (swapped, back, gave)):
            cells = cells[: mine * SLOT].reshape(mine, SLOT, channels)[:, :LAGS]
            stack.append(cells.astype(jnp.float32) * paired)
    return jnp.stack(received, axis=1), jnp.stack(swapped, axis=1)


def solution(mesh):
    in_specs = (
        P(("groups", "win"), "chan", None),
        P(("groups", "chan")),
        P(),
        P("groups"),
        P("groups", None),
    )
    out_specs = (
        P(("win", "sub"), None, None, ("groups", "chan")),
        P(("groups", "chan", "win", "sub"), None, None, None),
    )
    return jax.shard_map(
        on_device, mesh=mesh, in_specs=in_specs, out_specs=out_specs, check_vma=False
    )
```

time: 91.3 us -> 59.2 us (0.65)
  the two profiles are of different devices: /device:TPU:9 before, /device:TPU:0 now
where the time goes in v1:
time: 59.2 us; the launch traced here: 58.9 us
  Pallas kernels  42.3 us (71%)
  local copies, waits for them, and re-layouts  8.06 us (14%)
  between operations  7.14 us (12%)
  other arithmetic  1.34 us (2%)
    pallas_call x1, Pallas kernels, on_device(): pl.pallas_call(functools.partial(kernel, keys, wins, subs, mine, rows, cu...  42.3 us
    unnamed x12, local copies, waits for them, and re-layouts  3.41 us
    dynamic_slice x1, local copies, waits for them, and re-layouts, on_device(): gave = pair_list[block_at, offset].astype(jnp.float32)  1.74 us
    slice x1, local copies, waits for them, and re-layouts, on_device(): fwd[n]  1.64 us
    reshape x1, local copies, waits for them, and re-layouts, on_device(): channel_mask.reshape(1, channels)  1.27 us

profile of v1, /device:TPU:0, one launch (start us, length us, event | category | flops | bytes accessed | tf_op | source)
XLA Modules:
  0.0 58.9 jit_solution(6659200257252767262)
XLA Ops:
  0.7 1.7 %constant_dynamic-slice_fusion.4 = (s32[1,1]{1,0:T(1,128)}, s32[1,1]{1,0:T(1,128)}, s32[1,1]{1,0:T(1,128)}, s32[1,1]{1,0:T(1,128)}, s32[1,1]{1,0:T(1,128)}, /*in...) fusion(s32[4,5]{1,0:T(4,128)} %param.11, s32[]{:T(128)S(6)} %select_n.49, ...), kind=kLoop, calls=%fused_computation.34 | loop fusion | bytes 100 | tf_op jit(solution)/shard_map/dynamic_slice | solution.py:284
  3.1 1.3 %reshape.27.refs_2_ = s32[1,640]{1,0:T(1,128)} reshape(s32[640]{0:T(1024)} %param.8) | data formatting | bytes 5120 | tf_op jit(solution)/shard_map/reshape | solution.py:274
  4.4 42.3 %stacks.1 = (bf16[4,208,640]{2,1,0:T(8,128)(2,1)}, bf16[208,640]{1,0:T(8,128)(2,1)}, bf16[3,208,640]{2,1,0:T(8,128)(2,1)}) custom-call(s32[4]{0:T(128)} %refs_0_.1, bf16[640,1024]{1,0:T(8,128)(2,1)} %bitcast.66, s32[1,640]{1,0:T(1,128)} %reshape.27.refs_2_, s32[1,512]{1,0:T(1,128)} %bitcast.73, bf16[1024,1024]{1,0:T(8,128)(2,1)} %constant.48.clone.refs_4_, ...), custom_call_target="tpu_custom_call" | custom-call | tf_op jit(solution)/shard_map/stacks/pallas_call | solution.py:245
  46.7 0.0 copy-start
  46.7 1.6 %fusion.14 = (bf16[1,208,640]{2,1,0:T(8,128)(2,1)S(1)}, bf16[1,208,640]{2,1,0:T(8,128)(2,1)S(1)}, bf16[1,208,640]{2,1,0:T(8,128)(2,1)S(1)}, bf16[1,208,640]{2,1,...) fusion(bf16[4,208,640]{2,1,0:T(8,128)(2,1)} %get-tuple-element., ...), kind=kLoop, calls=%fused_computation.40 | loop fusion | bytes 3727360 | tf_op jit(solution)/shard_map/slice | solution.py:286
  48.4 0.4 fusion.5
  49.4 0.3 fusion.10
  50.3 0.0 copy-done
  50.4 0.3 fusion.9
  51.4 0.3 fusion.8
  52.3 0.3 fusion.7
  52.6 0.0 copy-start.1
  53.2 0.2 fusion.1
  54.1 0.3 fusion.13
  55.2 0.3 fusion.12
  56.2 0.0 copy-done.1
  56.2 0.3 fusion.11
  57.1 0.3 fusion.3
  57.4 0.0 copy-start.2
  57.4 1.5 %copy-done.2 = f32[2,5,101,640]{3,0,2,1:T(2,128)} copy-done((f32[2,5,101,640]{3,0,2,1:T(2,128)}, f32[2,5,101,640]{3,0,2,1:T(2,128)S(1)}, u32[]{:S(2)}) %copy-start.2) | copy-done | bytes 2585624
  (6 shorter events, 0.2 us)
Async XLA Ops:
  46.7 3.6 %copy-start = (bf16[208,640]{1,0:T(8,128)(2,1)S(1)}, bf16[208,640]{1,0:T(8,128)(2,1)}, u32[]{:S(2)}) copy-start(bf16[208,640]{1,0:T(8,128)(2,1)} %get-tuple-element.7) | copy-start | bytes 798724
  52.6 3.6 %copy-start.1 = (f32[2,5,101,640]{3,0,2,1:T(2,128)}, f32[2,5,101,640]{3,0,2,1:T(2,128)S(1)}, u32[]{:S(2)}) copy-start(f32[2,5,101,640]{3,0,2,1:T(2,128)S(1)} %fusion.7) | copy-start | bytes 7756804
  57.4 1.5 %copy-start.2 = (f32[2,5,101,640]{3,0,2,1:T(2,128)}, f32[2,5,101,640]{3,0,2,1:T(2,128)S(1)}, u32[]{:S(2)}) copy-start(f32[2,5,101,640]{3,0,2,1:T(2,128)S(1)} %fusion.3) | copy-start | bytes 7756804

commit v2 on v1

--- a/solution.py
+++ b/solution.py
@@ -45,12 +45,12 @@
 
 
 def kernel(keys, wins, subs, mine, rows, cuts, *refs):
-    phase_ref, traces, mask, widths, dft, lag = refs[:6]
-    fwd, own_back, far_back = refs[6:9]
+    phase_ref, pairs, traces, mask, widths, dft, lag = refs[:7]
+    fwd, back = refs[7:9]
     count = len(cuts)
     spectra = refs[9 : 9 + count]
     staged = refs[9 + count : 9 + 2 * count]
-    (weights, own_sources, sources, far_rows, near_rows,
+    (far_back, weights, own_sources, sources, far_rows, near_rows,
      s_send, s_recv, x_send, x_recv, c_send, c_recv, z_send, z_recv) = refs[9 + 2 * count :]
     samples = traces.shape[1]
     blocks = lax.axis_size("chan")
@@ -150,11 +150,13 @@
     over_x, over_c, over_z = [x_copies(0)], [], []
     for copy in over_x[0]:
         copy.start()
-    for i in range(1, count):
+    def feed(i):
         whiten(i)
         over_x.append(x_copies(i))
         for copy in over_x[i]:
             copy.start()
+
+    feed(1)
 
     def forward(i):
         over_c.append(c_copies(i))
@@ -165,19 +167,18 @@
     forward(0)
     for copy in s_copies:
         copy.wait_recv()
-    blank = rows - mine * SLOT
 
     def fill(target, at_row, sign, n, d):
+        cosines, sines = lag[0], lag[1] * sign
         re_parts, im_parts = [], []
         for v in range(mine):
             re = sources[n, d, v : v + 1, :NB]
             im = sources[n, d, v : v + 1, NB:]
-            cosines, sines = lag[0], lag[1] * sign
             re_parts.append(re * cosines - im * sines)
             im_parts.append(im * cosines + re * sines)
-        if blank:
-            re_parts.append(jnp.zeros((blank, NB), jnp.float32))
-            im_parts.append(jnp.zeros((blank, NB), jnp.float32))
+        if rows > mine * SLOT:
+            re_parts.append(jnp.zeros((rows - mine * SLOT, NB), jnp.float32))
+            im_parts.append(jnp.zeros((rows - mine * SLOT, NB), jnp.float32))
         base = d * 2 * NB
         span = slice(at_row, at_row + rows)
         target[span, base : base + NB] = jnp.concatenate(re_parts, axis=0).astype(jnp.bfloat16)
@@ -200,24 +201,35 @@
     def keep(i):
         start, width = cuts[i]
         lags = jnp.dot(near_rows[...], spectra[i][...], preferred_element_type=jnp.float32)
-        for n in range(len(keys)):
-            fwd[n, :, start : start + width] = lags[n * rows : (n + 1) * rows].astype(jnp.bfloat16)
-        own_back[:, start : start + width] = lags[len(keys) * rows :].astype(jnp.bfloat16)
+        for offset in range(OFFS):
+            n = keys.index((offset - REACH) % blocks)
+            got = pairs[lax.rem(block_at + 2 * blocks - offset + REACH, blocks), offset].astype(jnp.float32)
+            cells = lags[n * rows : (n + 1) * rows] * got
+            fwd[offset, :, start : start + width] = cells.astype(jnp.bfloat16)
+        gave = pairs[block_at, REACH].astype(jnp.float32)
+        back[REACH, :, start : start + width] = (lags[len(keys) * rows :] * gave).astype(jnp.bfloat16)
 
     send(0)
     for i in range(1, count):
-        forward(i)
-        if i == 1:
+        if i + 1 < count:
+            feed(i + 1)
+        else:
             for d in range(wins):
                 for n in range(len(keys)):
                     fill(near_rows, n * rows, 1.0, n, d)
                 fill(near_rows, len(keys) * rows, -1.0, 0, d)
+        forward(i)
         send(i)
     for i in range(count):
         keep(i)
-    for copies in over_z:
-        for copy in copies:
+    for i, (start, width) in enumerate(cuts):
+        for copy in over_z[i]:
             copy.wait()
+        for offset in range(OFFS):
+            n = keys.index((offset - REACH) % blocks)
+            if n:
+                gave = pairs[block_at, offset].astype(jnp.bfloat16)
+                back[offset, :, start : start + width] = far_back[n - 1, :, start : start + width] * gave
     for copies in over_x + over_c + [s_copies]:
         for copy in copies:
             copy.wait_send()
@@ -228,7 +240,6 @@
     subs = lax.axis_size("sub")
     wins = lax.axis_size("win")
     blocks = lax.axis_size("chan")
-    block_at = lax.axis_index("chan")
     mine = VS // (wins * subs)
     rows = -(-mine * SLOT // 16) * 16
     keys = [0]
@@ -242,18 +253,17 @@
     count = len(cuts)
     vmem = pl.BlockSpec(memory_space=pltpu.VMEM)
     dma = pltpu.SemaphoreType.DMA
-    fwd, own_back, far_back = pl.pallas_call(
+    smem = pl.BlockSpec(memory_space=pltpu.SMEM)
+    stack = jax.ShapeDtypeStruct((OFFS, rows, channels), jnp.bfloat16)
+    stacks = pl.pallas_call(
         functools.partial(kernel, keys, wins, subs, mine, rows, cuts),
-        out_shape=[
-            jax.ShapeDtypeStruct((nk, rows, channels), jnp.bfloat16),
-            jax.ShapeDtypeStruct((rows, channels), jnp.bfloat16),
-            jax.ShapeDtypeStruct((nk - 1, rows, channels), jnp.bfloat16),
-        ],
-        in_specs=[pl.BlockSpec(memory_space=pltpu.SMEM)] + [vmem] * 5,
-        out_specs=[vmem, vmem, pl.BlockSpec(memory_space=pl.ANY)],
+        out_shape=[stack, stack],
+        in_specs=[smem] * 2 + [vmem] * 5,
+        out_specs=[vmem, vmem],
         scratch_shapes=[pltpu.VMEM((depth, width), jnp.bfloat16) for _, width in cuts]
         + [pltpu.VMEM((nk - 1, rows, width), jnp.bfloat16) for _, width in cuts]
         + [
+            pltpu.VMEM((nk - 1, rows, channels), jnp.bfloat16),
             pltpu.VMEM((NB, NB), jnp.bfloat16),
             pltpu.VMEM((wins * subs, mine, 2 * NB), jnp.float32),
             pltpu.VMEM((nk, wins, mine, 2 * NB), jnp.float32),
@@ -270,23 +280,18 @@
         name="stacks",
     )(
         source_phase,
+        pair_list,
         traces.reshape(channels, samples),
         channel_mask.reshape(1, channels),
         smooth_width.reshape(1, NB),
         dft_rows(samples),
         lag_rows(samples, (NB * windows * wins) ** (-0.5)),
     )
-    received, swapped = [], []
-    for offset in range(OFFS):
-        key = (offset - REACH) % blocks
-        n = keys.index(key)
-        got = pair_list[(block_at - key) % blocks, offset].astype(jnp.float32)
-        gave = pair_list[block_at, offset].astype(jnp.float32)
-        back = own_back if n == 0 else far_back[n - 1]
-        for stack, cells, paired in ((received, fwd[n], got), (swapped, back, gave)):
-            cells = cells[: mine * SLOT].reshape(mine, SLOT, channels)[:, :LAGS]
-            stack.append(cells.astype(jnp.float32) * paired)
-    return jnp.stack(received, axis=1), jnp.stack(swapped, axis=1)
+    outs = []
+    for cells in stacks:
+        cells = cells[:, : mine * SLOT].reshape(OFFS, mine, SLOT, channels)[:, :, :LAGS]
+        outs.append(jnp.transpose(cells, (1, 0, 2, 3)).astype(jnp.float32))
+    return tuple(outs)
 
 
 def solution(mesh):

time: 59.2 us -> 50.1 us (0.85)
  between operations: 7.14 us -> 0.67 us
  local copies, waits for them, and re-layouts: 8.06 us -> 6.26 us
  Pallas kernels: 42.3 us -> 41.1 us
  other arithmetic: 1.34 us -> 1.95 us
    convert_element_type x0 -> x1, local copies, waits for them, and re-layouts: none -> 4.99 us  [on_device(): outs.append(jnp.transpose(cells, (1, 0, 2, 3)).astype(jnp.float32))]
    unnamed x12 -> x2, local copies, waits for them, and re-layouts: 3.41 us -> 0.01 us
    convert_element_type x0 -> x2, other arithmetic: none -> 1.95 us  [on_device(): outs.append(jnp.transpose(cells, (1, 0, 2, 3)).astype(jnp.float32))]
    dynamic_slice x1 -> x0, local copies, waits for them, and re-layouts: 1.74 us -> none  [on_device(): gave = pair_list[block_at, offset].astype(jnp.float32)]
    slice x1 -> x0, local copies, waits for them, and re-layouts: 1.64 us -> none  [on_device(): fwd[n]]
    pallas_call x1, Pallas kernels: 42.3 us -> 41.1 us  [on_device(): pl.pallas_call(functools.partial(kernel, keys, wins, subs, mine, rows, cu...]
where the time goes in v2:
time: 50.1 us; the launch traced here: 50 us
  Pallas kernels  41.1 us (82%)
  local copies, waits for them, and re-layouts  6.26 us (12%)
  other arithmetic  1.95 us (4%)
  between operations  0.67 us (1%)
    pallas_call x1, Pallas kernels, on_device(): pl.pallas_call(functools.partial(kernel, keys, wins, subs, mine, rows, cu...  41.1 us
    convert_element_type x1, local copies, waits for them, and re-layouts, on_device(): outs.append(jnp.transpose(cells, (1, 0, 2, 3)).astype(jnp.float32))  4.99 us
    convert_element_type x2, other arithmetic, on_device(): outs.append(jnp.transpose(cells, (1, 0, 2, 3)).astype(jnp.float32))  1.95 us
    reshape x1, local copies, waits for them, and re-layouts, on_device(): channel_mask.reshape(1, channels)  1.27 us

profile of v2, /device:TPU:0, one launch (start us, length us, event | category | flops | bytes accessed | tf_op | source)
XLA Modules:
  0.0 50.0 jit_solution(16637936512611194945)
XLA Ops:
  0.6 1.3 %reshape.20.refs_3_ = s32[1,640]{1,0:T(1,128)} reshape(s32[640]{0:T(1024)} %param.8) | data formatting | bytes 5120 | tf_op jit(solution)/shard_map/reshape | solution.py:285
  1.9 41.1 %stacks.1 = (bf16[5,208,640]{2,1,0:T(8,128)(2,1)}, bf16[5,208,640]{2,1,0:T(8,128)(2,1)}) custom-call(s32[4]{0:T(128)} %refs_0_.1, s32[4,5]{1,0:T(4,128)} %refs_1_.1, bf16[640,1024]{1,0:T(8,128)(2,1)} %bitcast.10, s32[1,640]{1,0:T(1,128)} %reshape.20.refs_3_, s32[1,512]{1,0:T(1,128)} %bitcast.11, bf16[1024,1024]{1,0:T(8,128)(2,1)} %constant.4.clone.refs_5_, ...), custom_call_target="tpu_custom_call" | custom-call | tf_op jit(solution)/shard_map/stacks/pallas_call | solution.py:258
  43.0 0.0 copy-start
  43.0 1.8 %slice_convert_fusion = f32[5,2,101,640]{3,2,1,0:T(8,128)S(1)} fusion(bf16[5,2,104,640]{3,2,1,0:T(8,128)(2,1)} %bitcast.9), kind=kLoop, calls=%fused_computation.2 | loop fusion | flops 646400 | bytes 3878400 | tf_op jit(solution)/shard_map/convert_element_type | solution.py:293
  44.8 0.0 copy-done
  44.8 0.2 slice_convert_fusion.1
  45.0 5.0 %copy_bitcast_fusion = (f32[2,5,101,640]{3,0,2,1:T(2,128)}, f32[2,5,101,640]{3,0,2,1:T(2,128)}) fusion(f32[5,2,101,640]{3,2,1,0:T(8,128)S(1)} %slice_convert_fusion, f32[5,2,101,640]{3,2,1,0:T(8,128)S(1)} %slice_convert_fusion.1), kind=kLoop, calls=%fused_computation | loop fusion | bytes 10342400 | tf_op jit(solution)/shard_map/convert_element_type | solution.py:293
Async XLA Ops:
  43.0 1.8 %copy-start = (bf16[5,208,640]{2,1,0:T(8,128)(2,1)S(1)}, bf16[5,208,640]{2,1,0:T(8,128)(2,1)}, u32[]{:S(2)}) copy-start(bf16[5,208,640]{2,1,0:T(8,128)(2,1)} %get-tuple-element.4) | copy-start | bytes 3993604

commit v3 on v2

--- a/solution.py
+++ b/solution.py
@@ -81,7 +81,7 @@
     def whiten(i):
         start, width = cuts[i]
         cut = traces[start : start + width, :]
-        scale = mask[:, start : start + width].astype(jnp.float32) * samples ** (-0.5)
+        scale = mask[start : start + width].reshape(1, width).astype(jnp.float32) * samples ** (-0.5)
         re = lax.dot_general(dft[:NB, :], cut, FAR, preferred_element_type=jnp.float32) * scale
         im = lax.dot_general(dft[NB:, :], cut, FAR, preferred_element_type=jnp.float32) * scale
         amplitude = jnp.sqrt(re * re + im * im)
@@ -282,7 +282,7 @@
         source_phase,
         pair_list,
         traces.reshape(channels, samples),
-        channel_mask.reshape(1, channels),
+        channel_mask,
         smooth_width.reshape(1, NB),
         dft_rows(samples),
         lag_rows(samples, (NB * windows * wins) ** (-0.5)),

time: 50.1 us -> 48.9 us (0.976)
  local copies, waits for them, and re-layouts: 6.26 us -> 4.99 us
    reshape x1 -> x0, local copies, waits for them, and re-layouts: 1.27 us -> none  [on_device(): channel_mask.reshape(1, channels)]
where the time goes in v3:
time: 48.9 us; the launch traced here: 48.7 us
  Pallas kernels  41.1 us (84%)
  local copies, waits for them, and re-layouts  4.99 us (10%)
  other arithmetic  1.95 us (4%)
  between operations  0.67 us (1%)
    pallas_call x1, Pallas kernels, on_device(): pl.pallas_call(functools.partial(kernel, keys, wins, subs, mine, rows, cu...  41.1 us
    convert_element_type x1, local copies, waits for them, and re-layouts, on_device(): outs.append(jnp.transpose(cells, (1, 0, 2, 3)).astype(jnp.float32))  4.99 us
    convert_element_type x2, other arithmetic, on_device(): outs.append(jnp.transpose(cells, (1, 0, 2, 3)).astype(jnp.float32))  1.95 us

profile of v3, /device:TPU:0, one launch (start us, length us, event | category | flops | bytes accessed | tf_op | source)
XLA Modules:
  0.0 48.7 jit_solution(17384265332278342859)
XLA Ops:
  0.6 41.1 %stacks.1 = (bf16[5,208,640]{2,1,0:T(8,128)(2,1)}, bf16[5,208,640]{2,1,0:T(8,128)(2,1)}) custom-call(s32[4]{0:T(128)} %refs_0_.1, s32[4,5]{1,0:T(4,128)} %refs_1_.1, bf16[640,1024]{1,0:T(8,128)(2,1)} %bitcast.10, s32[640]{0:T(1024)} %refs_3_.1, s32[1,512]{1,0:T(1,128)} %bitcast.11, bf16[1024,1024]{1,0:T(8,128)(2,1)} %constant.4.clone.refs_5_, ...), custom_call_target="tpu_custom_call" | custom-call | tf_op jit(solution)/shard_map/stacks/pallas_call | solution.py:258
  41.8 0.0 copy-start
  41.8 1.8 %slice_convert_fusion = f32[5,2,101,640]{3,2,1,0:T(8,128)S(1)} fusion(bf16[5,2,104,640]{3,2,1,0:T(8,128)(2,1)} %bitcast.9), kind=kLoop, calls=%fused_computation.2 | loop fusion | flops 646400 | bytes 3878400 | tf_op jit(solution)/shard_map/convert_element_type | solution.py:293
  43.5 0.0 copy-done
  43.6 0.2 slice_convert_fusion.1
  43.7 5.0 %copy_bitcast_fusion = (f32[2,5,101,640]{3,0,2,1:T(2,128)}, f32[2,5,101,640]{3,0,2,1:T(2,128)}) fusion(f32[5,2,101,640]{3,2,1,0:T(8,128)S(1)} %slice_convert_fusion, f32[5,2,101,640]{3,2,1,0:T(8,128)S(1)} %slice_convert_fusion.1), kind=kLoop, calls=%fused_computation | loop fusion | bytes 10342400 | tf_op jit(solution)/shard_map/convert_element_type | solution.py:293
Async XLA Ops:
  41.8 1.8 %copy-start = (bf16[5,208,640]{2,1,0:T(8,128)(2,1)S(1)}, bf16[5,208,640]{2,1,0:T(8,128)(2,1)}, u32[]{:S(2)}) copy-start(bf16[5,208,640]{2,1,0:T(8,128)(2,1)} %get-tuple-element.4) | copy-start | bytes 3993604
